TPU v7x, 32 devices: a whole 2x2x4 slice. The times are simulated.
32 devices in a mesh: clu: 4 (over z), row: 8 (over y, x, core).
Axes of the slice: x: 2, y: 2, z: 4, core: 2. Of those that a mesh axis runs over, the one named last changes fastest.
Arguments:
- rhs: float32 [256, 131072], P(None, ('clu', 'row')), may hold values from -6 to 6
- linv: float32 [512, 256, 256], P(('clu', 'row'))
- w_one: float32 [131072, 128], P(('clu', 'row')), may hold values from -1.5 to 1.5
- w_two: float32 [131072, 128], P(('clu', 'row')), may hold values from -1.5 to 1.5
- held: int32 [8], replicated, may hold values from 0 to 7, each once
- ranks: int32 [6], replicated, may hold values from 16 to 128, as said below
Outputs:
- solved: float32 [256, 131072], P(None, ('clu', 'row'))
Inputs may be any that keep to these rules, and one draw needn't show every extreme that they name: `ranks`: entries 0 to 3 are the level-one blocks of subtrees in order (two a subtree), the rest the level-two blocks; some entry equals 128. `held`: a permutation of the clusters.
All inputs are finite; a program needn't handle non-finite values.
Results may differ from a plain program's by a relative error of at most 0.0001.
Values sent between devices are 32-bit elements; how exact they have to be, the bound alone decides.
A program may use at most 128 MiB of HBM per device.

v0:
```python
import math

import jax
import jax.numpy as jnp
from jax import lax
from jax.sharding import PartitionSpec as P


def leaf_apply(values, inverse):
    blocks = inverse.shape[0]
    leaf_width = inverse.shape[1]
    pieces = values.reshape(values.shape[0], blocks, leaf_width).transpose(1, 0, 2)
    result = jnp.einsum("bcj,bij->bci", pieces, inverse, precision=lax.Precision.HIGHEST)
    return result.transpose(1, 0, 2).reshape(values.shape[0], blocks * leaf_width)


def shards(rhs, linv, w_one, w_two, held, ranks):
    highest = lax.Precision.HIGHEST
    local_rows = rhs.shape[1]
    clu_count = lax.axis_size("clu")
    row_count = lax.axis_size("row")
    half_rows = row_count // 2
    slot_count = 2 * clu_count
    tree_count = slot_count // 4
    rank_width = w_one.shape[1]
    scaling = 1.0 / math.sqrt(local_rows * half_rows)
    group_index = lax.axis_index("clu")
    row_index = lax.axis_index("row")
    upper_half = (row_index >= half_rows).astype(jnp.int32)
    own_slot = 2 * group_index + upper_half
    slot_ids = jnp.arange(slot_count)
    own_flag = slot_ids == own_slot
    own_weights = own_flag.astype(jnp.float32)
    own_cluster = jnp.sum(jnp.where(own_flag, held, 0))
    position = own_cluster % 4
    subtree = own_cluster // 4
    tree_weights = (jnp.arange(tree_count) == subtree).astype(jnp.float32)

    def chooser(offset):
        return (held == 4 * subtree + offset).astype(jnp.float32)

    block_ids = jnp.arange(ranks.shape[0])

    def mask_for(block_index):
        rank_value = jnp.sum(jnp.where(block_ids == block_index, ranks, 0))
        return (jnp.arange(rank_width) < rank_value).astype(jnp.float32)

    selector_one = chooser(0)
    selector_two = chooser(0) + chooser(1)
    selector_three = chooser(2)
    mask_one = mask_for(2 * subtree)
    mask_two = mask_for(slot_count // 2 + subtree)
    mask_three = mask_for(2 * subtree + 1)
    flag_one = (position == 1).astype(jnp.float32)
    flag_late = (position >= 2).astype(jnp.float32)
    flag_last = (position == 3).astype(jnp.float32)

    def couple(local_term, selector, rank_mask):
        share = jnp.sum(selector * own_weights)
        slotted = tree_weights[:, None, None] * (local_term * share)[None]
        summed_trees = lax.psum(slotted, ("clu", "row"))
        picked = jnp.einsum("g,gck->ck", tree_weights, summed_trees, precision=highest)
        return picked * rank_mask[None, :]

    current = rhs
    solved = leaf_apply(current, linv)
    coef_one = couple(jnp.dot(solved, w_one, precision=highest) * scaling, selector_one, mask_one)
    current = current - flag_one * jnp.dot(coef_one, w_one.T, precision=highest)
    solved = leaf_apply(current, linv)
    coef_two = couple(jnp.dot(solved, w_two, precision=highest) * scaling, selector_two, mask_two)
    current = current - flag_late * jnp.dot(coef_two, w_two.T, precision=highest)
    solved = leaf_apply(current, linv)
    coef_three = couple(
        jnp.dot(solved, w_one, precision=highest) * scaling, selector_three, mask_three
    )
    current = current - flag_last * jnp.dot(coef_three, w_one.T, precision=highest)
    solved = leaf_apply(current, linv)
    return solved


def solution(mesh):
    in_specs = (
        P(None, ("clu", "row")),
        P(("clu", "row"), None, None),
        P(("clu", "row"), None),
        P(("clu", "row"), None),
        P(),
        P(),
    )
    out_specs = P(None, ("clu", "row"))
    return jax.shard_map(shards, mesh=mesh, in_specs=in_specs, out_specs=out_specs, check_vma=False)
```

profile of v0, /device:TPU:1, one launch (start us, length us, event | category | flops | bytes accessed | tf_op | source)
XLA Modules:
  0.0 478.9 jit_solution(8841921524803487932)
XLA Ops:
  6.5 0.0 copy-start
  6.5 0.0 all-reduce.4.cloned.1.call-start
  6.5 1.4 select_reduce_fusion.1
  10.6 1.3 fusion.31
  12.6 12.0 %fusion.9 = f32[16,256,256]{1,2,0:T(8,128)S(1)} fusion(f32[16,256,256]{2,1,0:T(8,128)} %param.7, f32[32,16,8,256]{3,2,1,0:T(8,128)} %bitcast.70), kind=kOutput, calls=%fused_computation.16 | convolution fusion | flops 3221225472 | bytes 12582912 | tf_op jit(solution)/shard_map/bcj,bij->bci/dot_general | solution.py:13
  24.6 0.0 copy-start.7
  24.6 0.0 copy-done
  24.6 6.7 %convolution_multiply_fusion.5 = f32[256,128]{1,0:T(8,128)S(1)} fusion(f32[256,4096]{0,1:T(8,128)S(1)} %bitcast.72, f32[4096,128]{1,0:T(8,128)S(1)} %copy-done, f32[]{:T(128)S(6)} %mul.131), kind=kOutput, calls=%fused_computation.20 | convolution fusion | flops 1610645504 | bytes 6422532 | tf_op jit(solution)/shard_map/dot_general | solution.py:67
  31.4 0.8 broadcast_multiply_fusion.2
  32.2 0.0 all-reduce.4.cloned.1.call-update
  32.2 0.3 all-reduce.6.cloned.1.call-start
  32.5 0.0 copy-done.7
  32.5 0.7 fusion.32
  33.9 0.6 compare_convert_fusion.4
  34.5 125.7 %all-reduce.4.cloned.1.call-done = f32[2,256,128]{2,1,0:T(8,128)} async-done(((f32[2,256,128]{2,1,0:T(8,128)}), f32[2,256,128]{2,1,0:T(8,128)}) %all-reduce.4.cloned.1.call-update) | async-done | bytes 262160 | tf_op jit(solution)/shard_map/psum | solution.py:61
  160.3 1.6 fusion.15
  161.9 0.0 copy-start.1
  161.9 5.7 %fusion.2 = f32[256,4096]{1,0:T(8,128)S(1)} fusion(f32[256,4096]{1,0:T(8,128)} %param.6, f32[4096,128]{1,0:T(8,128)S(1)} %copy-done, f32[]{:T(128)S(6)} %convert_element_type.52, f32[256,128]{1,0:T(8,128)S(1)} %bitcast.78, f32[128]{0:T(128)S(1)} %compare_convert_fusion.4), kind=kOutput, calls=%fused_computation.5 | convolution fusion | flops 1612742656 | bytes 10617348 | tf_op jit(solution)/shard_map/dot_general | solution.py:68
  167.6 0.0 copy-start.4
  167.6 0.0 copy-done.1
  167.6 0.0 copy-start.6
  167.6 5.3 %fusion.7 = f32[16,256,256]{1,2,0:T(8,128)S(1)} fusion(f32[16,256,256]{2,1,0:T(8,128)S(1)} %copy-done.1, f32[32,16,8,256]{3,2,1,0:T(8,128)S(1)} %bitcast.68), kind=kOutput, calls=%fused_computation.13 | convolution fusion | flops 3221225472 | bytes 12582912 | tf_op jit(solution)/shard_map/bcj,bij->bci/dot_general | solution.py:13
  172.9 0.0 copy-done.4
  172.9 0.0 copy-done.6
  173.0 6.7 %convolution_multiply_fusion.4 = f32[256,128]{1,0:T(8,128)S(1)} fusion(f32[256,4096]{0,1:T(8,128)S(1)} %bitcast.73, f32[4096,128]{1,0:T(8,128)S(1)} %copy-done.6, f32[]{:T(128)S(6)} %mul.142), kind=kOutput, calls=%fused_computation.19 | convolution fusion | flops 1610645504 | bytes 6422532 | tf_op jit(solution)/shard_map/dot_general | solution.py:70
  179.7 0.8 broadcast_multiply_fusion.1
  180.5 0.0 all-reduce.6.cloned.1.call-update
  180.5 10.6 %all-reduce.8.cloned.1.call-start = ((), (), s32[]{:S(2)}) async-start(), calls=%async_computation.2 | async-start | bytes 524288 | tf_op jit(solution)/shard_map/psum | solution.py:61
  191.7 0.6 compare_convert_fusion.2
  192.3 114.0 %all-reduce.6.cloned.1.call-done = f32[2,256,128]{2,1,0:T(8,128)} async-done(((f32[2,256,128]{2,1,0:T(8,128)}), f32[2,256,128]{2,1,0:T(8,128)}) %all-reduce.6.cloned.1.call-update) | async-done | bytes 262160 | tf_op jit(solution)/shard_map/psum | solution.py:61
  306.3 1.7 fusion.13
  307.9 0.0 copy-start.2
  308.0 6.5 %fusion.1 = f32[256,4096]{1,0:T(8,128)S(1)} fusion(f32[256,4096]{1,0:T(8,128)} %copy-done.4, f32[4096,128]{1,0:T(8,128)} %param.9, f32[]{:T(128)S(6)} %convert_element_type.56, f32[256,128]{1,0:T(8,128)S(1)} %bitcast.77, f32[128]{0:T(128)S(1)} %compare_convert_fusion.2), kind=kOutput, calls=%fused_computation.3 | convolution fusion | flops 1612742656 | bytes 10617348 | tf_op jit(solution)/shard_map/dot_general | solution.py:71
  314.4 0.0 copy-start.5
  314.5 0.0 copy-done.2
  314.5 5.3 %fusion.5 = f32[16,256,256]{1,2,0:T(8,128)S(1)} fusion(f32[16,256,256]{2,1,0:T(8,128)S(1)} %copy-done.2, f32[32,16,8,256]{3,2,1,0:T(8,128)S(1)} %bitcast.69), kind=kOutput, calls=%fused_computation.10 | convolution fusion | flops 3221225472 | bytes 12582912 | tf_op jit(solution)/shard_map/bcj,bij->bci/dot_general | solution.py:13
  319.8 0.0 copy-done.5
  319.8 6.7 %convolution_multiply_fusion.3 = f32[256,128]{1,0:T(8,128)S(1)} fusion(f32[256,4096]{0,1:T(8,128)S(1)} %bitcast.74, f32[4096,128]{1,0:T(8,128)S(1)} %copy-done, f32[]{:T(128)S(6)} %mul.152), kind=kOutput, calls=%fused_computation.18 | convolution fusion | flops 1610645504 | bytes 6422532 | tf_op jit(solution)/shard_map/dot_general | solution.py:74
  326.5 0.8 broadcast_multiply_fusion
  327.3 0.0 all-reduce.8.cloned.1.call-update
  327.3 0.7 compare_convert_fusion
  328.0 125.1 %all-reduce.8.cloned.1.call-done = f32[2,256,128]{2,1,0:T(8,128)} async-done(((f32[2,256,128]{2,1,0:T(8,128)}), f32[2,256,128]{2,1,0:T(8,128)}) %all-reduce.8.cloned.1.call-update) | async-done | bytes 262160 | tf_op jit(solution)/shard_map/psum | solution.py:61
  453.1 1.9 fusion.11
  455.0 0.0 copy-start.3
  455.0 5.6 %fusion = f32[256,4096]{1,0:T(8,128)S(1)} fusion(f32[256,4096]{1,0:T(8,128)} %copy-done.5, f32[4096,128]{1,0:T(8,128)S(1)} %copy-done, f32[]{:T(128)S(6)} %convert_element_type.59, f32[256,128]{1,0:T(8,128)S(1)} %bitcast.76, f32[128]{0:T(128)S(1)} %compare_convert_fusion), kind=kOutput, calls=%fused_computation.1 | convolution fusion | flops 1612742656 | bytes 10617348 | tf_op jit(solution)/shard_map/dot_general | solution.py:76
  460.7 0.0 copy-done.3
  460.7 5.8 %fusion.3 = f32[16,256,256]{1,2,0:T(8,128)} fusion(f32[16,256,256]{2,1,0:T(8,128)S(1)} %copy-done.3, f32[32,16,8,256]{3,2,1,0:T(8,128)S(1)} %bitcast.71), kind=kOutput, calls=%fused_computation.7 | convolution fusion | flops 3221225472 | bytes 12582912 | tf_op jit(solution)/shard_map/bcj,bij->bci/dot_general | solution.py:13
  466.5 5.6 %copy.11 = f32[256,4096]{1,0:T(8,128)} copy(f32[256,4096]{0,1:T(8,128)} %bitcast.75) | data formatting | bytes 8388608 | tf_op jit(solution)/shard_map/reshape | solution.py:14
  (1 shorter events, 0.0 us)
Async XLA Ops:
  6.5 18.1 %copy-start = (f32[4096,128]{1,0:T(8,128)S(1)}, f32[4096,128]{1,0:T(8,128)}, u32[]{:S(2)}) copy-start(f32[4096,128]{1,0:T(8,128)} %param.8) | copy-start | bytes 6291460
  6.5 153.7 %all-reduce.4.cloned.1.call-start = ((), (), s32[]{:S(2)}) async-start(), calls=%async_computation | async-start | bytes 524288 | tf_op jit(solution)/shard_map/psum | solution.py:61
  24.6 7.9 %copy-start.7 = (s32[6]{0:T(128)S(1)}, s32[6]{0:T(128)}, u32[]{:S(2)}) copy-start(s32[6]{0:T(128)} %param.11) | copy-start | bytes 76
  32.2 274.1 %all-reduce.6.cloned.1.call-start = ((), (), s32[]{:S(2)}) async-start(), calls=%async_computation.1 | async-start | bytes 524288 | tf_op jit(solution)/shard_map/psum | solution.py:61
  161.9 5.7 %copy-start.1 = (f32[16,256,256]{2,1,0:T(8,128)S(1)}, f32[16,256,256]{2,1,0:T(8,128)}, u32[]{:S(2)}) copy-start(f32[16,256,256]{2,1,0:T(8,128)} %param.7) | copy-start | bytes 12582916
  167.6 5.3 %copy-start.4 = (f32[256,4096]{1,0:T(8,128)}, f32[256,4096]{1,0:T(8,128)S(1)}, u32[]{:S(2)}) copy-start(f32[256,4096]{1,0:T(8,128)S(1)} %fusion.2) | copy-start | bytes 12582916
  167.6 5.3 %copy-start.6 = (f32[4096,128]{1,0:T(8,128)S(1)}, f32[4096,128]{1,0:T(8,128)}, u32[]{:S(2)}) copy-start(f32[4096,128]{1,0:T(8,128)} %param.9) | copy-start | bytes 6291460
  180.5 272.6 %all-reduce.8.cloned.1.call-start = ((), (), s32[]{:S(2)}) async-start(), calls=%async_computation.2 | async-start | bytes 524288 | tf_op jit(solution)/shard_map/psum | solution.py:61
  307.9 6.5 %copy-start.2 = (f32[16,256,256]{2,1,0:T(8,128)S(1)}, f32[16,256,256]{2,1,0:T(8,128)}, u32[]{:S(2)}) copy-start(f32[16,256,256]{2,1,0:T(8,128)} %param.7) | copy-start | bytes 12582916
  314.4 5.3 %copy-start.5 = (f32[256,4096]{1,0:T(8,128)}, f32[256,4096]{1,0:T(8,128)S(1)}, u32[]{:S(2)}) copy-start(f32[256,4096]{1,0:T(8,128)S(1)} %fusion.1) | copy-start | bytes 12582916
  455.0 5.7 %copy-start.3 = (f32[16,256,256]{2,1,0:T(8,128)S(1)}, f32[16,256,256]{2,1,0:T(8,128)}, u32[]{:S(2)}) copy-start(f32[16,256,256]{2,1,0:T(8,128)} %param.7) | copy-start | bytes 12582916
Sparse Core Ops, SparseCore 0:
  32.3 127.8 all-reduce.3
  180.6 125.6 all-reduce.5
  327.5 125.6 all-reduce.7
where the time goes:
time: 488 us; the launch traced here: 479 us
  waiting for transfers between devices  365 us (75%)
  matrix products  71.6 us (15%)
  between operations  18 us (4%)
  starting transfers between devices  10.9 us (2%)
  other arithmetic  7.85 us (2%)
  local copies, waits for them, and re-layouts  5.64 us (1%)
    psum x3, waiting for transfers between devices, couple(): summed_trees = lax.psum(slotted, ('clu', 'row'))  365 us
    dot_general x4, matrix products, leaf_apply(): jnp.einsum('bcj,bij->bci', pieces, inverse, precision=lax.Precision.HIGHEST)  28.5 us
    dot_general x2, matrix products, shards(): jnp.dot(solved, w_one, precision=highest) * scaling  13.5 us
    psum x3, starting transfers between devices, couple(): summed_trees = lax.psum(slotted, ('clu', 'row'))  10.9 us
  transfers between devices with their start and end apart: 3, of which 3 were waited for; matrix products, arithmetic and copies ran while one was open for 1% of the time, Pallas kernels for 0%

commit v1 on v0

v1 whole, which is shorter than its diff:
```python
import math

import jax
import jax.numpy as jnp
from jax import lax
from jax.sharding import PartitionSpec as P

HIGH = lax.Precision.HIGH


def shards(rhs, linv, w_one, w_two, held, ranks):
    cols, local_rows = rhs.shape
    blocks, leaf, _ = linv.shape
    rank_width = w_one.shape[1]
    half_rows = lax.axis_size("row") // 2
    slot_count = 2 * lax.axis_size("clu")
    tree_count = slot_count // 4
    scaling = 1.0 / math.sqrt(local_rows * half_rows)
    own_slot = 2 * lax.axis_index("clu") + lax.axis_index("row") // half_rows
    own_cluster = jnp.sum(jnp.where(jnp.arange(slot_count) == own_slot, held, 0))
    position = own_cluster % 4
    subtree = own_cluster // 4
    tree_weights = (jnp.arange(tree_count) == subtree).astype(jnp.float32)

    def mask_for(block_index):
        rank_value = jnp.sum(jnp.where(jnp.arange(ranks.shape[0]) == block_index, ranks, 0))
        return (jnp.arange(rank_width) < rank_value).astype(jnp.float32)[None, :]

    flag = [(position == p).astype(jnp.float32) for p in range(4)]

    weights = jnp.concatenate([w_one, w_two], axis=1)
    leaf_weights = weights.reshape(blocks, leaf, 2 * rank_width)
    pieces = rhs.reshape(cols, blocks, leaf)
    base = jnp.einsum("cbj,bij->cbi", pieces, linv, precision=HIGH)
    spread = jnp.einsum("bij,bjk->bik", linv, leaf_weights, precision=HIGH)
    sums = jnp.dot(base.reshape(cols, local_rows), weights, precision=HIGH) * scaling
    spread = spread.reshape(local_rows, 2 * rank_width)
    second = position == 1
    left = jnp.where(second, spread[:, :rank_width], spread[:, rank_width:])
    right = jnp.where(second, w_two, w_one)
    cross = jnp.einsum("rk,rm->km", left, right, precision=HIGH) * scaling

    one, two = sums[:, :rank_width], sums[:, rank_width:]
    message = jnp.concatenate(
        [flag[0] * one, (flag[0] + flag[1]) * two, flag[2] * one, flag[1] * cross, flag[2] * cross],
        axis=0,
    )
    total = lax.psum(tree_weights[:, None, None] * message[None], ("clu", "row"))
    mine = jnp.sum(tree_weights[:, None, None] * total, axis=0)
    sum_one, sum_two, sum_three = (mine[i * cols : (i + 1) * cols] for i in range(3))
    cross_two, cross_three = (
        mine[3 * cols + i * rank_width : 3 * cols + (i + 1) * rank_width] for i in range(2)
    )
    coef_one = sum_one * mask_for(2 * subtree)
    coef_two = sum_two - jnp.dot(coef_one, cross_two, precision=HIGH)
    coef_two = coef_two * mask_for(slot_count // 2 + subtree)
    coef_three = sum_three - jnp.dot(coef_two, cross_three, precision=HIGH)
    coef_three = coef_three * mask_for(2 * subtree + 1)
    coefs = jnp.concatenate(
        [flag[1] * coef_one + flag[3] * coef_three, (flag[2] + flag[3]) * coef_two], axis=1
    )
    fixes = jnp.einsum("ck,rk->cr", coefs, spread, precision=HIGH)
    return base.reshape(cols, local_rows) - fixes


def solution(mesh):
    in_specs = (
        P(None, ("clu", "row")),
        P(("clu", "row"), None, None),
        P(("clu", "row"), None),
        P(("clu", "row"), None),
        P(),
        P(),
    )
    out_specs = P(None, ("clu", "row"))
    return jax.shard_map(shards, mesh=mesh, in_specs=in_specs, out_specs=out_specs, check_vma=False)
```

time: 488 us -> 188 us (0.39); the launches traced: 479 us -> 186 us
  waiting for transfers between devices: 365 us -> 124 us
  matrix products: 71.6 us -> 30.1 us
  starting transfers between devices: 10.9 us -> 0.01 us
    psum x3 -> x1, waiting for transfers between devices: 365 us -> 124 us  [shards(): lax.psum(tree_weights[:, None, None] * message[None], ('clu', 'row'))]
    dot_general x13 -> x7, matrix products: 71.6 us -> 30.1 us  [the longest x1 8.96 us: shards(): fixes = jnp.einsum('ck,rk->cr', coefs, spread, precision=HIGH)]
    psum x3 -> x1, starting transfers between devices: 10.9 us -> 0.01 us  [shards(): lax.psum(tree_weights[:, None, None] * message[None], ('clu', 'row'))]
  transfers between devices with their start and end apart: 3 -> 1, of which waited for: 3 -> 1; matrix products, arithmetic and copies ran while one was open for 1% -> 5% of each run, Pallas kernels for 0% -> 0%
where the time goes in v1:
time: 188 us; the launch traced here: 186 us
  waiting for transfers between devices  124 us (66%)
  matrix products  30.1 us (16%)
  between operations  16.2 us (9%)
  local copies, waits for them, and re-layouts  8.95 us (5%)
  other arithmetic  6.59 us (4%)
    psum x1, waiting for transfers between devices, shards(): lax.psum(tree_weights[:, None, None] * message[None], ('clu', 'row'))  124 us
    dot_general x1, matrix products, shards(): fixes = jnp.einsum('ck,rk->cr', coefs, spread, precision=HIGH)  8.96 us
    dot_general x1, matrix products, shards(): spread = jnp.einsum('bij,bjk->bik', linv, leaf_weights, precision=HIGH)  7.65 us
    reshape x1, local copies, waits for them, and re-layouts, shards(): return base.reshape(cols, local_rows) - fixes  5.84 us
    dot_general x1, matrix products, shards(): base = jnp.einsum('cbj,bij->cbi', pieces, linv, precision=HIGH)  5.31 us
    dot_general x1, matrix products, shards(): cross = jnp.einsum('rk,rm->km', left, right, precision=HIGH) * scaling  4.06 us
  transfers between devices with their start and end apart: 1, of which 1 were waited for; matrix products, arithmetic and copies ran while one was open for 5% of the time, Pallas kernels for 0%

profile of v1, /device:TPU:1, one launch (start us, length us, event | category | flops | bytes accessed | tf_op | source)
XLA Modules:
  0.0 186.1 jit_solution(18188946085965173614)
XLA Ops:
  6.5 0.0 copy-start.4
  6.5 0.0 all-reduce.2.cloned.1.call-start
  6.5 1.4 fusion.19
  10.6 0.0 copy-start.2
  10.6 1.9 %constant_dynamic-update-slice_fusion.1 = f32[4096,256]{1,0:T(8,128)S(1)} fusion(f32[4096,128]{1,0:T(8,128)} %param.8), kind=kLoop, calls=%fused_computation.33 | loop fusion | bytes 4194304
  12.5 0.0 copy-done.4
  12.5 0.2 constant_dynamic-update-slice_fusion
  12.7 0.0 copy-start.1
  12.7 0.7 copy-done.2
  13.4 5.3 %fusion = f32[16,256,256]{2,1,0:T(8,128)S(1)} fusion(f32[16,256,256]{2,1,0:T(8,128)S(1)} %copy-done.2, f32[32,16,8,256]{3,2,1,0:T(8,128)} %bitcast.23), kind=kOutput, calls=%fused_computation.1 | convolution fusion | flops 1610612736 | bytes 12582912 | tf_op jit(solution)/shard_map/cbj,bij->cbi/dot_general | solution.py:34
  18.7 0.0 copy-start
  18.8 0.0 copy-done.1
  18.8 3.6 %convolution_multiply_fusion = f32[256,256]{1,0:T(8,128)S(1)} fusion(f32[256,4096]{0,1:T(8,128)S(1)} %bitcast.18, f32[4096,256]{1,0:T(8,128)S(1)} %constant_dynamic-update-slice_fusion), kind=kOutput, calls=%fused_computation.8 | convolution fusion | flops 1610678272 | bytes 8650752 | tf_op jit(solution)/shard_map/dot_general | solution.py:36
  22.4 0.0 copy-done
  22.4 0.0 copy-start.3
  22.4 7.6 %fusion.25 = f32[16,256,256]{1,2,0:T(8,128)} fusion(f32[16,256,256]{2,1,0:T(8,128)} %bitcast.22, f32[16,256,256]{2,1,0:T(8,128)} %param.7), kind=kOutput, calls=%fused_computation.48 | convolution fusion | flops 1610612736 | bytes 12582912 | tf_op jit(solution)/shard_map/bij,bjk->bik/dot_general | solution.py:35
  30.1 0.0 copy-done.3
  30.1 4.1 %multiply_dynamic-update-slice_fusion.3 = (f32[1024,128]{1,0:T(8,128)S(1)}, f32[128,128]{1,0:T(8,128)S(1)}) fusion(f32[1024,128]{1,0:T(8,128)S(1)} %multiply_dynamic-update-slice_fusion, f32[]{:T(128)S(6)} %mul.121, f32[4096,128]{1,0:T(8,128)} %param.9, f32[4096,128]{1,0:T(8,128)S(1)} %copy-done.3, pred[]{:T(512)S(6)} %eq.51, f32[4096,256]{1,0:T(8,128)} %bitcast.20), kind=kOutput, calls=%fused_computation.31 | convolution fusion | flops 403718144 | bytes 8521216 | tf_op jit(solution)/shard_map/rk,rm->km/dot_general | solution.py:41
  34.2 1.1 broadcast_multiply_fusion
  35.3 0.0 all-reduce.2.cloned.1.call-update
  35.3 0.0 copy-start.5
  35.3 5.8 %copy.13 = f32[256,4096]{1,0:T(8,128)} copy(f32[256,4096]{0,1:T(8,128)} %bitcast.19) | data formatting | bytes 8388608 | tf_op jit(solution)/shard_map/reshape | solution.py:63
  41.2 0.0 copy-done.5
  41.2 0.7 fusion.22
  41.9 0.7 compare_convert_fusion.2
  42.5 1.2 compare_convert_fusion
  43.7 124.2 %all-reduce.2.cloned.1.call-done = f32[2,1024,128]{2,1,0:T(8,128)} async-done(((f32[2,1024,128]{2,1,0:T(8,128)}), f32[2,1024,128]{2,1,0:T(8,128)}) %all-reduce.2.cloned.1.call-update) | async-done | bytes 1048592 | tf_op jit(solution)/shard_map/psum | solution.py:48
  168.0 1.4 multiply_reduce_fusion
  169.4 0.1 copy.14
  169.5 0.1 copy.16
  169.6 0.1 copy.15
  169.7 0.3 broadcast_multiply_fusion.1
  170.1 0.3 fusion.9
  170.3 9.0 %convolution_subtract_fusion = f32[256,4096]{1,0:T(8,128)} fusion(f32[256,4096]{1,0:T(8,128)} %copy.13, f32[4096,256]{1,0:T(8,128)} %bitcast.21, f32[256,128]{0,1:T(8,128)S(1)} %get-tuple-element.13, f32[256,128]{0,1:T(8,128)S(1)} %fusion.9), kind=kOutput, calls=%fused_computation | convolution fusion | flops 1611726848 | bytes 12845056 | tf_op jit(solution)/shard_map/ck,rk->cr/dot_general | solution.py:62
  (6 shorter events, 0.1 us)
Async XLA Ops:
  6.5 6.0 %copy-start.4 = (f32[4096,128]{1,0:T(8,128)S(1)}, f32[4096,128]{1,0:T(8,128)}, u32[]{:S(2)}) copy-start(f32[4096,128]{1,0:T(8,128)} %param.9) | copy-start | bytes 6291460
  6.5 161.4 %all-reduce.2.cloned.1.call-start = ((), (), s32[]{:S(2)}) async-start(), calls=%async_computation | async-start | bytes 2097152 | tf_op jit(solution)/shard_map/psum | solution.py:48
  10.6 2.8 %copy-start.2 = (f32[16,256,256]{2,1,0:T(8,128)S(1)}, f32[16,256,256]{2,1,0:T(8,128)}, u32[]{:S(2)}) copy-start(f32[16,256,256]{2,1,0:T(8,128)} %param.7) | copy-start | bytes 12582916
  12.7 6.0 %copy-start.1 = (f32[4096,256]{1,0:T(8,128)}, f32[4096,256]{1,0:T(8,128)S(1)}, u32[]{:S(2)}) copy-start(f32[4096,256]{1,0:T(8,128)S(1)} %constant_dynamic-update-slice_fusion) | copy-start | bytes 12582916
  18.7 3.6 %copy-start = (f32[16,256,256]{2,1,0:T(8,128)}, f32[16,256,256]{2,1,0:T(8,128)S(1)}, u32[]{:S(2)}) copy-start(f32[16,256,256]{2,1,0:T(8,128)S(1)} %fusion) | copy-start | bytes 12582916
  22.4 7.7 %copy-start.3 = (f32[4096,128]{1,0:T(8,128)S(1)}, f32[4096,128]{1,0:T(8,128)}, u32[]{:S(2)}) copy-start(f32[4096,128]{1,0:T(8,128)} %param.8) | copy-start | bytes 6291460
  35.3 5.9 %copy-start.5 = (s32[6]{0:T(128)S(1)}, s32[6]{0:T(128)}, u32[]{:S(2)}) copy-start(s32[6]{0:T(128)} %param.11) | copy-start | bytes 76
Sparse Core Ops, SparseCore 0:
  35.4 132.4 all-reduce.1

commit v2 on v1

v2 whole, which is shorter than its diff:
```python
import functools
import math

import jax
import jax.numpy as jnp
from jax import lax
from jax.experimental import pallas as pl
from jax.experimental.pallas import tpu as pltpu
from jax.sharding import PartitionSpec as P

MESH = pl.DeviceIdType.MESH
NN = (((1,), (0,)), ((), ()))
NT = (((1,), (1,)), ((), ()))
TN = (((0,), (0,)), ((), ()))


def split(x):
    high = x.astype(jnp.bfloat16)
    return high, (x - high.astype(jnp.float32)).astype(jnp.bfloat16)


def dot3(a, b, dims):
    def one(x, y):
        return lax.dot_general(x, y, dims, preferred_element_type=jnp.float32)

    return one(a[0], b[0]) + (one(a[0], b[1]) + one(a[1], b[0]))


def kernel(
    groups, members, chunks, step,
    held, ranks, rhs, linv, w_one, w_two, out,
    x_buf, l_buf, w_buf, l_hi, l_lo, w_hi, w_lo, s_hi, s_lo,
    g_acc, g_recv, g_sum, g_all, m_acc, m_recv, m_all, m_full, k_send, k_full, k_hi, k_lo,
    in_sems, out_sems, m1_s, m1_r, m2_s, m2_r, m3_s, m3_r, g1_s, g1_r, g2_s, g2_r, k1_s, k1_r, k2_s, k2_r,
):
    cols, rows = x_buf.shape
    blocks, leaf, _ = l_buf.shape
    rank = w_one.shape[1]
    trees = groups // 4
    passes = blocks // step
    width = step * leaf
    scaling = 1.0 / math.sqrt(rows * members)
    clu, row = lax.axis_index("clu"), lax.axis_index("row")
    group = 2 * clu + row // members
    member = row % members
    base = chunks * (group // chunks)
    chunk = group % chunks

    def device_of(g, q):
        return (g // 2, (g % 2) * members + q)

    def loads(c):
        span = pl.ds(pl.multiple_of(c * width, width), width)
        some = pl.ds(c * step, step)
        return (
            pltpu.make_async_copy(linv.at[some], l_buf.at[some], in_sems.at[0, c]),
            pltpu.make_async_copy(w_one.at[span], w_buf.at[span, pl.ds(0, rank)], in_sems.at[1, c]),
            pltpu.make_async_copy(w_two.at[span], w_buf.at[span, pl.ds(rank, rank)], in_sems.at[2, c]),
            pltpu.make_async_copy(rhs.at[:, span], x_buf.at[:, span], in_sems.at[3, c]),
        )

    for c in range(passes):
        for copy in loads(c)[:3]:
            copy.start()
    for c in range(passes):
        loads(c)[3].start()

    other_members = [(member + k) % members for k in range(1, members)]
    other_groups = [(group + k) % groups for k in range(1, groups)]
    block_groups = [base + (chunk + k) % chunks for k in range(1, chunks)]

    barrier = pltpu.get_barrier_semaphore()
    for q in other_members:
        pl.semaphore_signal(barrier, inc=1, device_id=device_of(group, q), device_id_type=MESH)
    for g in other_groups:
        pl.semaphore_signal(barrier, inc=1, device_id=device_of(g, member), device_id_type=MESH)

    def remote(src, dst, send, recv, g, q):
        return pltpu.make_async_remote_copy(
            src_ref=src, dst_ref=dst, send_sem=send, recv_sem=recv,
            device_id=device_of(g, q), device_id_type=MESH,
        )

    sends = []

    def send(*args):
        copy = remote(*args)
        copy.start()
        sends.append(copy)

    position = held[group] % 4
    second = jnp.where(position == 1, 1.0, 0.0).astype(jnp.float32)

    m_acc[...] = jnp.zeros_like(m_acc)
    g_acc[...] = jnp.zeros_like(g_acc)

    def spread(c, carry):
        for copy in loads(c)[:3]:
            copy.wait()
        total = jnp.zeros((rank, rank), jnp.float32)
        for i in range(step):
            b = c * step + i
            span = pl.ds(pl.multiple_of(b * leaf, leaf), leaf)
            weights = w_buf[span, :]
            inverse = split(l_buf[b])
            pair = split(weights)
            l_hi[b], l_lo[b] = inverse
            w_hi[b], w_lo[b] = pair
            result = dot3(inverse, pair, NN)
            s_hi[b], s_lo[b] = split(result)
            left = second * result[:, :rank] + (1.0 - second) * result[:, rank:]
            right = second * weights[:, rank:] + (1.0 - second) * weights[:, :rank]
            total = total + dot3(split(left), split(right), TN)
        m_acc[...] += total.reshape(m_acc.shape)
        return carry

    def solve(c, carry):
        loads(c)[3].wait()
        total = jnp.zeros((cols, 2 * rank), jnp.float32)
        for i in range(step):
            b = c * step + i
            span = pl.ds(pl.multiple_of(b * leaf, leaf), leaf)
            result = dot3(split(x_buf[:, span]), (l_hi[b], l_lo[b]), NT)
            x_buf[:, span] = result
            total = total + dot3(split(result), (w_hi[b], w_lo[b]), NN)
        g_acc[...] += total.reshape(g_acc.shape)
        return carry

    lax.fori_loop(0, passes, spread, 0)
    pl.semaphore_wait(barrier, members - 1 + groups - 1)
    for q in other_members:
        send(m_acc.at[q], m_recv.at[member], m1_s.at[q], m1_r.at[member], group, q)

    lax.fori_loop(0, passes // 2, solve, 0)

    total = m_acc[member]
    for q in other_members:
        remote(m_acc.at[q], m_recv.at[q], m1_s.at[q], m1_r.at[q], group, q).wait_recv()
        total = total + m_recv[q]
    m_all[group] = total * scaling
    for g in other_groups:
        send(m_all.at[group], m_all.at[group], m2_s.at[g], m2_r.at[group], g, member)

    lax.fori_loop(passes // 2, passes, solve, 0)

    for q in other_members:
        send(g_acc.at[q], g_recv.at[member], g1_s.at[q], g1_r.at[member], group, q)

    def weight(g, cluster):
        return jnp.where(held[g] == cluster, 1.0, 0.0).astype(jnp.float32)

    for g in other_groups:
        remote(m_all.at[g], m_all.at[g], m2_s.at[g], m2_r.at[g], g, member).wait_recv()
    for t in range(trees):
        for kind in range(2):
            picked = jnp.zeros(m_all.shape[1:], jnp.float32)
            for g in range(groups):
                picked = picked + weight(g, 4 * t + 1 + kind) * m_all[g]
            m_full[member, 2 * t + kind] = picked
    for q in other_members:
        send(m_full.at[member], m_full.at[member], m3_s.at[q], m3_r.at[member], group, q)

    total = g_acc[member]
    for q in other_members:
        remote(g_acc.at[q], g_recv.at[q], g1_s.at[q], g1_r.at[q], group, q).wait_recv()
        total = total + g_recv[q]
    g_sum[...] = (total * scaling).reshape(g_sum.shape)
    g_all[group] = g_sum[chunk]
    for g in other_groups:
        send(g_sum.at[g % chunks], g_all.at[group], g2_s.at[g], g2_r.at[group], g, member)

    lanes = lax.broadcasted_iota(jnp.int32, (1, rank), 1)

    def mask(index):
        return jnp.where(lanes < ranks[index], 1.0, 0.0).astype(jnp.float32)

    for q in other_members:
        remote(m_full.at[q], m_full.at[q], m3_s.at[q], m3_r.at[q], group, q).wait_recv()
    crosses = [
        split(jnp.concatenate([m_full[q, s] for q in range(members)], axis=0)) for s in range(2 * trees)
    ]
    for g in other_groups:
        remote(g_all.at[g], g_all.at[g], g2_s.at[g], g2_r.at[g], g, member).wait_recv()
    coefs = []
    for t in range(trees):
        zero = jnp.zeros((g_all.shape[1], rank), jnp.float32)
        one, two, three = zero, zero, zero
        for g in range(groups):
            first, last = g_all[g, :, :rank], g_all[g, :, rank:]
            one = one + weight(g, 4 * t) * first
            two = two + (weight(g, 4 * t) + weight(g, 4 * t + 1)) * last
            three = three + weight(g, 4 * t + 2) * first
        one = one * mask(2 * t)
        two = (two - dot3(split(one), crosses[2 * t], NN)) * mask(2 * trees + t)
        three = (three - dot3(split(two), crosses[2 * t + 1], NN)) * mask(2 * t + 1)
        coefs.append((one, two, three))
    for g in range(groups):
        first = jnp.zeros((g_all.shape[1], rank), jnp.float32)
        last = first
        for t in range(trees):
            one, two, three = coefs[t]
            first = first + weight(g, 4 * t + 1) * one + weight(g, 4 * t + 3) * three
            last = last + (weight(g, 4 * t + 2) + weight(g, 4 * t + 3)) * two
        k_send[g, :, :rank] = first
        k_send[g, :, rank:] = last
    k_full[member, chunk] = k_send[group]
    for g in block_groups:
        send(k_send.at[g], k_full.at[member, chunk], k1_s.at[g], k1_r.at[chunk], g, member)
    for g in block_groups:
        c = g % chunks
        remote(k_send.at[g], k_full.at[member, c], k1_s.at[g], k1_r.at[c], g, member).wait_recv()
    for q in other_members:
        send(k_full.at[member], k_full.at[member], k2_s.at[q], k2_r.at[member], group, q)
    for q in other_members:
        remote(k_full.at[q], k_full.at[q], k2_s.at[q], k2_r.at[q], group, q).wait_recv()
    k_hi[...], k_lo[...] = split(k_full[...].reshape(cols, 2 * rank))

    def store(c):
        span = pl.ds(pl.multiple_of(c * width, width), width)
        return pltpu.make_async_copy(x_buf.at[:, span], out.at[:, span], out_sems.at[c])

    def update(c, carry):
        coef = (k_hi[...], k_lo[...])
        for i in range(step):
            b = c * step + i
            span = pl.ds(pl.multiple_of(b * leaf, leaf), leaf)
            x_buf[:, span] = x_buf[:, span] - dot3(coef, (s_hi[b], s_lo[b]), NT)
        store(c).start()
        return carry

    lax.fori_loop(0, passes, update, 0)
    for copy in sends:
        copy.wait_send()
    for c in range(passes):
        store(c).wait()


def shards(rhs, linv, w_one, w_two, held, ranks):
    cols, rows = rhs.shape
    blocks, leaf, _ = linv.shape
    rank = w_one.shape[1]
    groups = 2 * lax.axis_size("clu")
    members = lax.axis_size("row") // 2
    trees = groups // 4
    share = cols // members
    chunks = min(groups, share // 8)
    piece = share // chunks
    part = rank // members
    step = 2
    f32, bf16 = jnp.float32, jnp.bfloat16
    leaf_shape = (blocks, leaf, leaf)
    weight_shape = (blocks, leaf, 2 * rank)
    dma = pltpu.SemaphoreType.DMA
    return pl.pallas_call(
        functools.partial(kernel, groups, members, chunks, step),
        out_shape=jax.ShapeDtypeStruct(rhs.shape, f32),
        in_specs=[pl.BlockSpec(memory_space=pltpu.SMEM)] * 2 + [pl.BlockSpec(memory_space=pl.ANY)] * 4,
        out_specs=pl.BlockSpec(memory_space=pl.ANY),
        scratch_shapes=[
            pltpu.VMEM((cols, rows), f32),
            pltpu.VMEM(leaf_shape, f32),
            pltpu.VMEM((rows, 2 * rank), f32),
            pltpu.VMEM(leaf_shape, bf16),
            pltpu.VMEM(leaf_shape, bf16),
            pltpu.VMEM(weight_shape, bf16),
            pltpu.VMEM(weight_shape, bf16),
            pltpu.VMEM(weight_shape, bf16),
            pltpu.VMEM(weight_shape, bf16),
            pltpu.VMEM((members, share, 2 * rank), f32),
            pltpu.VMEM((members, share, 2 * rank), f32),
            pltpu.VMEM((chunks, piece, 2 * rank), f32),
            pltpu.VMEM((groups, piece, 2 * rank), f32),
            pltpu.VMEM((members, part, rank), f32),
            pltpu.VMEM((members, part, rank), f32),
            pltpu.VMEM((groups, part, rank), f32),
            pltpu.VMEM((members, 2 * trees, part, rank), f32),
            pltpu.VMEM((groups, piece, 2 * rank), f32),
            pltpu.VMEM((members, chunks, piece, 2 * rank), f32),
            pltpu.VMEM((cols, 2 * rank), bf16),
            pltpu.VMEM((cols, 2 * rank), bf16),
            dma((4, blocks // step)),
            dma((blocks // step,)),
            dma((members,)), dma((members,)),
            dma((groups,)), dma((groups,)),
            dma((members,)), dma((members,)),
            dma((members,)), dma((members,)),
            dma((groups,)), dma((groups,)),
            dma((groups,)), dma((chunks,)),
            dma((members,)), dma((members,)),
        ],
        compiler_params=pltpu.CompilerParams(
            collective_id=0, has_side_effects=True, vmem_limit_bytes=48 * 1024 * 1024
        ),
    )(held, ranks, rhs, linv, w_one, w_two)


def solution(mesh):
    in_specs = (
        P(None, ("clu", "row")),
        P(("clu", "row"), None, None),
        P(("clu", "row"), None),
        P(("clu", "row"), None),
        P(),
        P(),
    )
    out_specs = P(None, ("clu", "row"))
    return jax.shard_map(shards, mesh=mesh, in_specs=in_specs, out_specs=out_specs, check_vma=False)
```

time: 188 us -> 52.4 us (0.28)
  waiting for transfers between devices: 124 us -> 0 us
  Pallas kernels: 0 us -> 43 us
  matrix products: 30.1 us -> 0 us
  between operations: 16.2 us -> 0.01 us
  other arithmetic: 6.59 us -> 0 us
    psum x1 -> x0, waiting for transfers between devices: 124 us -> none  [shards(): lax.psum(tree_weights[:, None, None] * message[None], ('clu', 'row'))]
    pallas_call x0 -> x1, Pallas kernels: none -> 43 us  [shards(): pl.pallas_call(functools.partial(kernel, groups, members, chunks, step),...]
    dot_general x7 -> x0, matrix products: 30.1 us -> none  [the longest x1 8.96 us: shards(): fixes = jnp.einsum('ck,rk->cr', coefs, spread, precision=HIGH)]
    unnamed x16 -> x9, local copies, waits for them, and re-layouts: 2.93 us -> 9.15 us
    reshape x1 -> x0, local copies, waits for them, and re-layouts: 5.84 us -> none  [shards(): return base.reshape(cols, local_rows) - fixes]
    reduce_sum x3 -> x0, other arithmetic: 3.56 us -> none  [the longest x1 1.44 us: shards(): jnp.sum(jnp.where(jnp.arange(slot_count) == own_slot, held, 0))]
  transfers between devices with their start and end apart: 1 -> 0, of which waited for: 1 -> 0; matrix products, arithmetic and copies ran while one was open for 5% -> 0% of each run, Pallas kernels for 0% -> 0%
where the time goes in v2:
time: 52.4 us; the launch traced here: 52.1 us
  Pallas kernels  43 us (82%)
  local copies, waits for them, and re-layouts  9.15 us (17%)
    pallas_call x1, Pallas kernels, shards(): pl.pallas_call(functools.partial(kernel, groups, members, chunks, step),...  43 us
    unnamed x9, local copies, waits for them, and re-layouts  9.15 us

profile of v2, /device:TPU:1, one launch (start us, length us, event | category | flops | bytes accessed | tf_op | source)
XLA Modules:
  0.0 52.1 jit_solution(17934829375643414082)
XLA Ops:
  0.0 0.0 copy-start
  0.0 1.6 %copy-done = f32[4096,128]{1,0:T(8,128)S(1)} copy-done((f32[4096,128]{1,0:T(8,128)S(1)}, f32[4096,128]{1,0:T(8,128)}, u32[]{:S(2)}) %copy-start) | copy-done | bytes 2097176
  1.6 0.0 copy-start.1
  1.6 1.6 %copy-done.1 = f32[4096,128]{1,0:T(8,128)S(1)} copy-done((f32[4096,128]{1,0:T(8,128)S(1)}, f32[4096,128]{1,0:T(8,128)}, u32[]{:S(2)}) %copy-start.1) | copy-done | bytes 2097176
  3.2 0.0 copy-start.2
  3.2 0.7 %copy-done.2 = s32[8]{0:T(128)S(1)} copy-done((s32[8]{0:T(128)S(1)}, s32[8]{0:T(128)}, u32[]{:S(2)}) %copy-start.2) | copy-done | bytes 56
  3.8 0.0 copy-start.3
  3.8 0.7 %copy-done.3 = s32[6]{0:T(128)S(1)} copy-done((s32[6]{0:T(128)S(1)}, s32[6]{0:T(128)}, u32[]{:S(2)}) %copy-start.3) | copy-done | bytes 48
  4.5 43.0 %shard_map.64 = f32[256,4096]{1,0:T(8,128)} custom-call(s32[8]{0:T(128)S(1)} %copy-done.2, s32[6]{0:T(128)S(1)} %copy-done.3, f32[256,4096]{1,0:T(8,128)} %rhs.1, f32[16,256,256]{2,1,0:T(8,128)} %linv.1, f32[4096,128]{1,0:T(8,128)S(1)} %copy-done, f32[4096,128]{1,0:T(8,128)S(1)} %copy-done.1), custom_call_target="tpu_custom_call" | custom-call | tf_op jit(solution)/shard_map/pallas_call | solution.py:254
  47.5 4.7 %copy.8 = f32[256,4096]{1,0:T(8,128)} copy(f32[256,4096]{1,0:T(8,128)} %shard_map.64) | data formatting | bytes 8388608
Async XLA Ops:
  0.0 1.6 %copy-start = (f32[4096,128]{1,0:T(8,128)S(1)}, f32[4096,128]{1,0:T(8,128)}, u32[]{:S(2)}) copy-start(f32[4096,128]{1,0:T(8,128)} %w_one.1) | copy-start | bytes 6291460
  1.6 1.6 %copy-start.1 = (f32[4096,128]{1,0:T(8,128)S(1)}, f32[4096,128]{1,0:T(8,128)}, u32[]{:S(2)}) copy-start(f32[4096,128]{1,0:T(8,128)} %w_two.1) | copy-start | bytes 6291460
  3.2 0.7 %copy-start.2 = (s32[8]{0:T(128)S(1)}, s32[8]{0:T(128)}, u32[]{:S(2)}) copy-start(s32[8]{0:T(128)} %held.1) | copy-start | bytes 100
  3.8 0.7 %copy-start.3 = (s32[6]{0:T(128)S(1)}, s32[6]{0:T(128)}, u32[]{:S(2)}) copy-start(s32[6]{0:T(128)} %ranks.1) | copy-start | bytes 76

commit v3 on v2

--- a/solution.py
+++ b/solution.py
@@ -28,9 +28,9 @@
 
 def kernel(
     groups, members, chunks, step,
-    held, ranks, rhs, linv, w_one, w_two, out,
+    held, ranks, rhs, linv, w_one, w_two, z_out, hi_out, lo_out, k_hi, k_lo,
     x_buf, l_buf, w_buf, l_hi, l_lo, w_hi, w_lo, s_hi, s_lo,
-    g_acc, g_recv, g_sum, g_all, m_acc, m_recv, m_all, m_full, k_send, k_full, k_hi, k_lo,
+    g_acc, g_recv, g_sum, g_all, m_acc, m_recv, m_all, m_full, k_send, k_full,
     in_sems, out_sems, m1_s, m1_r, m2_s, m2_r, m3_s, m3_r, g1_s, g1_r, g2_s, g2_r, k1_s, k1_r, k2_s, k2_r,
 ):
     cols, rows = x_buf.shape
@@ -57,6 +57,15 @@
             pltpu.make_async_copy(w_one.at[span], w_buf.at[span, pl.ds(0, rank)], in_sems.at[1, c]),
             pltpu.make_async_copy(w_two.at[span], w_buf.at[span, pl.ds(rank, rank)], in_sems.at[2, c]),
             pltpu.make_async_copy(rhs.at[:, span], x_buf.at[:, span], in_sems.at[3, c]),
+        )
+
+    def stores(c):
+        span = pl.ds(pl.multiple_of(c * width, width), width)
+        some = pl.ds(c * step, step)
+        return (
+            pltpu.make_async_copy(x_buf.at[:, span], z_out.at[:, span], out_sems.at[0, c]),
+            pltpu.make_async_copy(s_hi.at[some], hi_out.at[some], out_sems.at[1, c]),
+            pltpu.make_async_copy(s_lo.at[some], lo_out.at[some], out_sems.at[2, c]),
         )
 
     for c in range(passes):
@@ -112,6 +121,8 @@
             right = second * weights[:, rank:] + (1.0 - second) * weights[:, :rank]
             total = total + dot3(split(left), split(right), TN)
         m_acc[...] += total.reshape(m_acc.shape)
+        for copy in stores(c)[1:]:
+            copy.start()
         return carry
 
     def solve(c, carry):
@@ -124,6 +135,7 @@
             x_buf[:, span] = result
             total = total + dot3(split(result), (w_hi[b], w_lo[b]), NN)
         g_acc[...] += total.reshape(g_acc.shape)
+        stores(c)[0].start()
         return carry
 
     lax.fori_loop(0, passes, spread, 0)
@@ -215,24 +227,19 @@
         remote(k_full.at[q], k_full.at[q], k2_s.at[q], k2_r.at[q], group, q).wait_recv()
     k_hi[...], k_lo[...] = split(k_full[...].reshape(cols, 2 * rank))
 
-    def store(c):
-        span = pl.ds(pl.multiple_of(c * width, width), width)
-        return pltpu.make_async_copy(x_buf.at[:, span], out.at[:, span], out_sems.at[c])
-
-    def update(c, carry):
-        coef = (k_hi[...], k_lo[...])
-        for i in range(step):
-            b = c * step + i
-            span = pl.ds(pl.multiple_of(b * leaf, leaf), leaf)
-            x_buf[:, span] = x_buf[:, span] - dot3(coef, (s_hi[b], s_lo[b]), NT)
-        store(c).start()
-        return carry
-
-    lax.fori_loop(0, passes, update, 0)
     for copy in sends:
         copy.wait_send()
     for c in range(passes):
-        store(c).wait()
+        for copy in stores(c):
+            copy.wait()
+
+
+def update(base, high, low, coef_high, coef_low, out):
+    leaf = high.shape[1]
+    coef = (coef_high[...], coef_low[...])
+    for i in range(high.shape[0]):
+        span = pl.ds(i * leaf, leaf)
+        out[:, span] = base[:, span] - dot3(coef, (high[i], low[i]), NT)
 
 
 def shards(rhs, linv, w_one, w_two, held, ranks):
@@ -251,11 +258,18 @@
     leaf_shape = (blocks, leaf, leaf)
     weight_shape = (blocks, leaf, 2 * rank)
     dma = pltpu.SemaphoreType.DMA
-    return pl.pallas_call(
+    hbm = pl.BlockSpec(memory_space=pl.ANY)
+    base, high, low, coef_high, coef_low = pl.pallas_call(
         functools.partial(kernel, groups, members, chunks, step),
-        out_shape=jax.ShapeDtypeStruct(rhs.shape, f32),
+        out_shape=[
+            jax.ShapeDtypeStruct(rhs.shape, f32),
+            jax.ShapeDtypeStruct(weight_shape, bf16),
+            jax.ShapeDtypeStruct(weight_shape, bf16),
+            jax.ShapeDtypeStruct((cols, 2 * rank), bf16),
+            jax.ShapeDtypeStruct((cols, 2 * rank), bf16),
+        ],
         in_specs=[pl.BlockSpec(memory_space=pltpu.SMEM)] * 2 + [pl.BlockSpec(memory_space=pl.ANY)] * 4,
-        out_specs=pl.BlockSpec(memory_space=pl.ANY),
+        out_specs=[hbm] * 3 + [pl.BlockSpec(memory_space=pltpu.VMEM)] * 2,
         scratch_shapes=[
             pltpu.VMEM((cols, rows), f32),
             pltpu.VMEM(leaf_shape, f32),
@@ -276,10 +290,8 @@
             pltpu.VMEM((members, 2 * trees, part, rank), f32),
             pltpu.VMEM((groups, piece, 2 * rank), f32),
             pltpu.VMEM((members, chunks, piece, 2 * rank), f32),
-            pltpu.VMEM((cols, 2 * rank), bf16),
-            pltpu.VMEM((cols, 2 * rank), bf16),
             dma((4, blocks // step)),
-            dma((blocks // step,)),
+            dma((3, blocks // step)),
             dma((members,)), dma((members,)),
             dma((groups,)), dma((groups,)),
             dma((members,)), dma((members,)),
@@ -289,9 +301,19 @@
             dma((members,)), dma((members,)),
         ],
         compiler_params=pltpu.CompilerParams(
-            collective_id=0, has_side_effects=True, vmem_limit_bytes=48 * 1024 * 1024
+            collective_id=0, has_side_effects=True, vmem_limit_bytes=60 * 1024 * 1024
         ),
     )(held, ranks, rhs, linv, w_one, w_two)
+    wide = pl.BlockSpec((cols, step * leaf), lambda c: (0, c))
+    stack = pl.BlockSpec((step, leaf, 2 * rank), lambda c: (c, 0, 0))
+    whole = pl.BlockSpec((cols, 2 * rank), lambda c: (0, 0))
+    return pl.pallas_call(
+        update,
+        grid=(blocks // step,),
+        out_shape=jax.ShapeDtypeStruct(rhs.shape, f32),
+        in_specs=[wide, stack, stack, whole, whole],
+        out_specs=wide,
+    )(base, high, low, coef_high, coef_low)
 
 
 def solution(mesh):

time: 52.4 us -> 49.1 us (0.937)
  local copies, waits for them, and re-layouts: 9.15 us -> 0 us
  Pallas kernels: 43 us -> 48.8 us
    unnamed x9 -> x0, local copies, waits for them, and re-layouts: 9.15 us -> none
    pallas_call x0 -> x1, Pallas kernels: none -> 8.84 us  [shards(): pl.pallas_call(update, grid=(blocks // step,), out_shape=jax.ShapeDtypeSt...]
    pallas_call x1, Pallas kernels: 43 us -> 39.9 us  [shards(): pl.pallas_call(functools.partial(kernel, groups, members, chunks, step),...]
where the time goes in v3:
time: 49.1 us; the launch traced here: 48.8 us
  Pallas kernels  48.8 us (99%)
    pallas_call x1, Pallas kernels, shards(): pl.pallas_call(functools.partial(kernel, groups, members, chunks, step),...  39.9 us
    pallas_call x1, Pallas kernels, shards(): pl.pallas_call(update, grid=(blocks // step,), out_shape=jax.ShapeDtypeSt...  8.84 us

profile of v3, /device:TPU:1, one launch (start us, length us, event | category | flops | bytes accessed | tf_op | source)
XLA Modules:
  0.0 48.8 jit_solution(16616574426326816568)
XLA Ops:
  0.0 39.9 %shard_map.64 = (f32[256,4096]{1,0:T(8,128)}, bf16[16,256,256]{2,1,0:T(8,128)(2,1)}, bf16[16,256,256]{2,1,0:T(8,128)(2,1)}, bf16[256,256]{1,0:T(8,128)(2,1)}, bf16[256,256]{1,0:T(8,128)(2,1)}) custom-call(s32[8]{0:T(128)} %held.1, s32[6]{0:T(128)} %ranks.1, f32[256,4096]{1,0:T(8,128)} %rhs.1, f32[16,256,256]{2,1,0:T(8,128)} %linv.1, f32[4096,128]{1,0:T(8,128)} %w_one.1, ...), custom_call_target="tpu_custom_call" | custom-call | tf_op jit(solution)/shard_map/pallas_call | solution.py:262
  39.9 8.8 %shard_map.65 = f32[256,4096]{1,0:T(8,128)} custom-call(f32[256,4096]{1,0:T(8,128)} %get-tuple-element.10.base, bf16[16,256,256]{2,1,0:T(8,128)(2,1)} %get-tuple-element.11.high, bf16[16,256,256]{2,1,0:T(8,128)(2,1)} %get-tuple-element.12.low, bf16[256,256]{1,0:T(8,128)(2,1)} %get-tuple-element.13.coef_high, bf16[256,256]{1,0:T(8,128)(2,1)} %get-tuple-element.14.coef_low), custom_call_target="tpu_custom_call" | custom-call | tf_op jit(solution)/shard_map/pallas_call | solution.py:310

commit v4 on v3

--- a/solution.py
+++ b/solution.py
@@ -234,12 +234,44 @@
             copy.wait()
 
 
-def update(base, high, low, coef_high, coef_low, out):
-    leaf = high.shape[1]
-    coef = (coef_high[...], coef_low[...])
-    for i in range(high.shape[0]):
-        span = pl.ds(i * leaf, leaf)
-        out[:, span] = base[:, span] - dot3(coef, (high[i], low[i]), NT)
+def update(step, base, high, low, coef_high, coef_low, out, x_buf, s_hi, s_lo, in_sems, out_sems):
+    blocks, leaf, _ = s_hi.shape
+    passes = blocks // step
+    width = step * leaf
+
+    def loads(c):
+        span = pl.ds(pl.multiple_of(c * width, width), width)
+        some = pl.ds(c * step, step)
+        return (
+            pltpu.make_async_copy(high.at[some], s_hi.at[some], in_sems.at[0, c]),
+            pltpu.make_async_copy(low.at[some], s_lo.at[some], in_sems.at[1, c]),
+            pltpu.make_async_copy(base.at[:, span], x_buf.at[:, span], in_sems.at[2, c]),
+        )
+
+    def store(c):
+        span = pl.ds(pl.multiple_of(c * width, width), width)
+        return pltpu.make_async_copy(x_buf.at[:, span], out.at[:, span], out_sems.at[c])
+
+    for c in range(passes):
+        for copy in loads(c):
+            copy.start()
+    coef = jnp.concatenate([coef_high[...], coef_high[...], coef_low[...]], axis=1)
+
+    def work(c, carry):
+        for copy in loads(c):
+            copy.wait()
+        for i in range(step):
+            b = c * step + i
+            span = pl.ds(pl.multiple_of(b * leaf, leaf), leaf)
+            bases = jnp.concatenate([s_hi[b], s_lo[b], s_hi[b]], axis=1)
+            fix = lax.dot_general(coef, bases, NT, preferred_element_type=jnp.float32)
+            x_buf[:, span] = x_buf[:, span] - fix
+        store(c).start()
+        return carry
+
+    lax.fori_loop(0, passes, work, 0)
+    for c in range(passes):
+        store(c).wait()
 
 
 def shards(rhs, linv, w_one, w_two, held, ranks):
@@ -304,15 +336,19 @@
             collective_id=0, has_side_effects=True, vmem_limit_bytes=60 * 1024 * 1024
         ),
     )(held, ranks, rhs, linv, w_one, w_two)
-    wide = pl.BlockSpec((cols, step * leaf), lambda c: (0, c))
-    stack = pl.BlockSpec((step, leaf, 2 * rank), lambda c: (c, 0, 0))
-    whole = pl.BlockSpec((cols, 2 * rank), lambda c: (0, 0))
     return pl.pallas_call(
-        update,
-        grid=(blocks // step,),
+        functools.partial(update, step),
         out_shape=jax.ShapeDtypeStruct(rhs.shape, f32),
-        in_specs=[wide, stack, stack, whole, whole],
-        out_specs=wide,
+        in_specs=[hbm] * 3 + [pl.BlockSpec(memory_space=pltpu.VMEM)] * 2,
+        out_specs=hbm,
+        scratch_shapes=[
+            pltpu.VMEM((cols, rows), f32),
+            pltpu.VMEM(weight_shape, bf16),
+            pltpu.VMEM(weight_shape, bf16),
+            dma((3, blocks // step)),
+            dma((blocks // step,)),
+        ],
+        compiler_params=pltpu.CompilerParams(vmem_limit_bytes=60 * 1024 * 1024),
     )(base, high, low, coef_high, coef_low)
 
 

time: 49.1 us -> 46.9 us (0.955)
  Pallas kernels: 48.8 us -> 46.7 us
    pallas_call x1, Pallas kernels: 8.84 us -> 6.81 us  [shards(): pl.pallas_call(functools.partial(update, step), out_shape=jax.ShapeDtypeS...]
where the time goes in v4:
time: 46.9 us; the launch traced here: 46.7 us
  Pallas kernels  46.7 us (100%)
    pallas_call x1, Pallas kernels, shards(): pl.pallas_call(functools.partial(kernel, groups, members, chunks, step),...  39.9 us
    pallas_call x1, Pallas kernels, shards(): pl.pallas_call(functools.partial(update, step), out_shape=jax.ShapeDtypeS...  6.81 us

profile of v4, /device:TPU:1, one launch (start us, length us, event | category | flops | bytes accessed | tf_op | source)
XLA Modules:
  0.0 46.7 jit_solution(14011788009765329994)
XLA Ops:
  0.0 39.9 %shard_map.64 = (f32[256,4096]{1,0:T(8,128)}, bf16[16,256,256]{2,1,0:T(8,128)(2,1)}, bf16[16,256,256]{2,1,0:T(8,128)(2,1)}, bf16[256,256]{1,0:T(8,128)(2,1)}, bf16[256,256]{1,0:T(8,128)(2,1)}) custom-call(s32[8]{0:T(128)} %held.1, s32[6]{0:T(128)} %ranks.1, f32[256,4096]{1,0:T(8,128)} %rhs.1, f32[16,256,256]{2,1,0:T(8,128)} %linv.1, f32[4096,128]{1,0:T(8,128)} %w_one.1, ...), custom_call_target="tpu_custom_call" | custom-call | tf_op jit(solution)/shard_map/pallas_call | solution.py:294
  39.9 6.8 %shard_map.65 = f32[256,4096]{1,0:T(8,128)} custom-call(f32[256,4096]{1,0:T(8,128)} %get-tuple-element.10.base, bf16[16,256,256]{2,1,0:T(8,128)(2,1)} %get-tuple-element.11.high, bf16[16,256,256]{2,1,0:T(8,128)(2,1)} %get-tuple-element.12.low, bf16[256,256]{1,0:T(8,128)(2,1)} %get-tuple-element.13.coef_high, bf16[256,256]{1,0:T(8,128)(2,1)} %get-tuple-element.14.coef_low), custom_call_target="tpu_custom_call" | custom-call | tf_op jit(solution)/shard_map/pallas_call | solution.py:339
